TPU v7x, 32 devices: a whole 2x2x4 slice. The times are simulated.
32 devices in a mesh: tm: 8 (over y, x, core), panel: 4 (over z).
Axes of the slice: x: 2, y: 2, z: 4, core: 2. Of those that a mesh axis runs over, the one named last changes fastest.
Arguments:
- series: float32 [48, 2048], P(None, 'tm'), may hold values from -20 to 20, as said below
- start_block: float32 [18432, 64], P(('tm', 'panel')), may hold values from -6 to 6
Outputs:
- covariance: float32 [18432, 18432], P(('tm', 'panel'))
- basis: float32 [7, 18432, 64], P(None, ('tm', 'panel'))
- diag_blocks: float32 [6, 64, 64], replicated
- off_blocks: float32 [7, 64, 64], replicated
Inputs may be any that keep to these rules, and one draw needn't show every extreme that they name: `series`: each channel has its own scale.
All inputs are finite; a program needn't handle non-finite values.
Results may differ from a plain program's by a relative error of at most 0.0003.
Values sent between devices are 32-bit elements; how exact they have to be, the bound alone decides.
No kernel may reach another device: no remote copies, remote signals or barrier semaphores. Data moves between devices by JAX's collectives and lax.ppermute only.
A program may use at most 192 MiB of HBM per device.

v0:
```python
import math

import jax
import jax.numpy as jnp
from jax import lax
from jax.sharding import PartitionSpec as P

M = 384
ITERS = 6


exact_precision = lax.Precision.HIGHEST


def passed_along(block, axis, distance):
    devices = range(lax.axis_size(axis))
    route = [(i - distance, i) for i in devices if i - distance in devices]
    return lax.ppermute(block, axis, route)


def lag_block(local_rows, extended, first_lag, lag_width):
    day_count = local_rows.shape[1]
    span = day_count + lag_width - 1
    segment = extended[:, first_lag : first_lag + span]
    repeated = jnp.tile(segment, (1, lag_width + 1))[:, : lag_width * (span + 1)]
    windows = repeated.reshape(segment.shape[0], lag_width, span + 1)[:, :, :day_count]
    return jnp.einsum(
        "lt,mjt->ljm",
        local_rows,
        windows,
        precision=exact_precision,
        preferred_element_type=jnp.float32,
    )


def lag_products(local_rows, extended):
    lag_width = math.gcd(M, 128)
    parts_list = [
        lag_block(local_rows, extended, first_lag, lag_width)
        for first_lag in range(0, M, lag_width)
    ]
    return jnp.concatenate(parts_list, axis=1)


def local(series, start_block):
    channels, day_count = series.shape
    tm_size = lax.axis_size("tm")
    panel_size = lax.axis_size("panel")
    total_days = day_count * tm_size
    reach_hops = (M - 1 + day_count - 1) // day_count
    pieces = [series]
    moving = series
    for distance in range(reach_hops):
        moving = passed_along(moving, "tm", -1)
        pieces.append(moving)
    extended = jnp.concatenate(pieces, axis=1)
    summed = lax.psum(lag_products(series, extended), "tm")
    counts = (total_days - jnp.arange(M)).astype(jnp.float32)
    normed = summed / counts[None, :, None]
    two_sided = jnp.concatenate([jnp.transpose(normed, (2, 1, 0))[:, :0:-1, :], normed], axis=1)
    lags_here = M // (tm_size * panel_size)
    block_index = lax.axis_index("tm") * panel_size + lax.axis_index("panel")
    row_list = []
    for offset in range(lags_here):
        lag_index = block_index * lags_here + offset
        window = lax.dynamic_slice(
            two_sided, (jnp.int32(0), M - 1 - lag_index, jnp.int32(0)), (channels, M, channels)
        )
        row_list.append(window.reshape(channels, M * channels))
    covariance = jnp.concatenate(row_list, axis=0)

    def inner(left, right):
        return jnp.dot(left.T, right, precision=exact_precision, preferred_element_type=jnp.float32)

    factor = jnp.linalg.cholesky(lax.psum(inner(start_block, start_block), ("tm", "panel")))
    current = jax.scipy.linalg.solve_triangular(factor, start_block.T, lower=True).T
    previous = jnp.zeros_like(current)
    upper = factor.T
    basis_list = [current]
    diagonal_list = []
    upper_list = [upper]
    for iteration in range(ITERS):
        work = jnp.dot(
            covariance,
            lax.all_gather(current, ("tm", "panel"), axis=0, tiled=True),
            precision=exact_precision,
            preferred_element_type=jnp.float32,
        )
        if iteration > 0:
            work = work - jnp.dot(
                previous, upper.T, precision=exact_precision, preferred_element_type=jnp.float32
            )
        diagonal, work_gram, basis_gram = lax.psum(
            (inner(current, work), inner(work, work), inner(current, current)), ("tm", "panel")
        )
        work = work - jnp.dot(
            current, diagonal, precision=exact_precision, preferred_element_type=jnp.float32
        )
        cross_term = jnp.dot(
            diagonal.T, diagonal, precision=exact_precision, preferred_element_type=jnp.float32
        )
        weighted = jnp.dot(
            diagonal.T,
            jnp.dot(
                basis_gram, diagonal, precision=exact_precision, preferred_element_type=jnp.float32
            ),
            precision=exact_precision,
            preferred_element_type=jnp.float32,
        )
        gram_matrix = work_gram - 2.0 * cross_term + weighted
        factor = jnp.linalg.cholesky(gram_matrix)
        upper = factor.T
        previous = current
        current = jax.scipy.linalg.solve_triangular(factor, work.T, lower=True).T
        basis_list.append(current)
        diagonal_list.append(diagonal)
        upper_list.append(upper)
    return (covariance, jnp.stack(basis_list), jnp.stack(diagonal_list), jnp.stack(upper_list))


def solution(mesh):
    placed = (P(None, "tm"), P(("tm", "panel"), None))
    return jax.shard_map(
        local,
        mesh=mesh,
        in_specs=placed,
        out_specs=(P(("tm", "panel"), None), P(None, ("tm", "panel"), None), P(), P()),
        check_vma=False,
    )
```

profile of v0, /device:TPU:0, one launch (start us, length us, event | category | flops | bytes accessed | tf_op | source)
XLA Modules:
  0.0 1534.1 jit_solution(18036461764195849786)
XLA Ops:
  58.0 14.1 collective-permute-start.1
  107.5 46.1 %psum.141 = f32[64,64]{0,1:T(8,128)S(1)} all-reduce(f32[64,64]{0,1:T(8,128)S(1)} %fusion.85), channel_id=1, replica_groups=mesh['tm'=8,'panel'=4] {'tm','panel'}, use_global_device_ids=true, to_apply=%region_1.0 | all-reduce | flops 4096 | bytes 32768 | tf_op jit(solution)/shard_map/psum | solution.py:75
  168.9 20.2 %all-reduce.8.cloned.1.call-done = f32[48,384,48]{1,0,2:T(8,128)} async-done(((f32[48,384,48]{1,0,2:T(8,128)}), f32[48,384,48]{1,0,2:T(8,128)}) %all-reduce.8.cloned.1.call-update) | async-done | bytes 3538960 | tf_op jit(solution)/shard_map/psum | solution.py:57
  208.3 18.9 %fusion.6 = (f32[48,384,48]{1,0,2:T(8,128)}, f32[48,384,48]{1,0,2:T(8,128)}, f32[48,384,48]{1,0,2:T(8,128)}, f32[48,384,48]{1,0,2:T(8,128)}, f32[48,384,48]{1,0,2:T(8,128)}, /*index=5*/f32[48,384,48]{1,0,2:T(8,128)}) fusion(s32[]{:T(128)S(6)} %select_n.50, f32[48,383,48]{1,0,2:T(8,128)} %slice.72, f32[48,384,48]{1,0,2:T(8,128)S(1)} %copy-done.3, ...), kind=kLoop, calls=%fused_computation.30 | loop fusion | flops 5308416 | bytes 28302360 | tf_op jit(solution)/shard_map/concatenate | solution.py:60
  234.9 10.3 reshape.81
  275.0 10.2 reshape.83
  293.0 10.4 reshape.84
  311.1 10.2 reshape.85
  321.4 27.2 %fusion.17 = (f32[48,384,48]{1,0,2:T(8,128)}, f32[48,384,48]{1,0,2:T(8,128)}, f32[48,384,48]{1,0,2:T(8,128)}, f32[48,384,48]{1,0,2:T(8,128)}, f32[48,384,48]{1,0,2:T(8,128)}, /*index=5*/f32[48,384,48]{1,0,2:T(8,128)}) fusion(s32[]{:T(128)S(6)} %select_n.49, f32[48,383,48]{1,0,2:T(8,128)} %slice.72, f32[48,384,48]{1,0,2:T(8,128)} %copy-done.2, ...), kind=kLoop, calls=%fused_computation.41 | loop fusion | flops 5308416 | bytes 28302360 | tf_op jit(solution)/shard_map/concatenate | solution.py:60
  356.4 10.2 reshape.86
  374.4 10.3 reshape.87
  392.5 10.4 reshape.88
  451.3 10.2 reshape.90
  469.3 10.3 reshape.91
  487.3 10.6 reshape.92
  524.9 43.1 %fusion.86 = f32[576,64]{0,1:T(8,128)S(1)} fusion(f32[576,18432]{1,0:T(8,128)} %constant_dynamic-update-slice_fusion.2, f32[18432,64]{0,1:T(8,128)} %reshape.94), kind=kOutput, calls=%fused_computation.202 | convolution fusion | flops 8153726976 | bytes 47333376 | tf_op jit(solution)/shard_map/dot_general | solution.py:83
  568.7 46.3 %all-reduce.5 = (f32[64,64]{1,0:T(8,128)S(1)}, f32[64,64]{0,1:T(8,128)S(1)}, f32[64,64]{1,0:T(8,128)S(1)}) all-reduce(f32[64,64]{1,0:T(8,128)S(1)} %fusion.88, f32[64,64]{0,1:T(8,128)S(1)} %fusion.87, f32[64,64]{1,0:T(8,128)S(1)} %copy-done.24), channel_id=1, replica_groups=mesh['tm'=8,'panel'=4] {'tm','panel'}, use_global_device_ids=true, to_apply=%region_5.0 | all-reduce | flops 12288 | bytes 98304 | tf_op jit(solution)/shard_map/psum | solution.py:93
  630.6 63.8 %all-gather.15.cloned.1.call-done = f32[32,576,64]{1,2,0:T(8,128)} async-done(((f32[1,576,64]{1,2,0:T(8,128)}), f32[32,576,64]{1,2,0:T(8,128)}) %all-gather.15.cloned.1.call-update) | async-done | bytes 4718608 | tf_op jit(solution)/shard_map/all_gather | solution.py:85
  708.8 43.1 %fusion.91 = f32[576,64]{0,1:T(8,128)S(1)} fusion(f32[576,18432]{1,0:T(8,128)} %constant_dynamic-update-slice_fusion.2, f32[18432,64]{0,1:T(8,128)} %reshape.96), kind=kOutput, calls=%fused_computation.207 | convolution fusion | flops 8153726976 | bytes 47333376 | tf_op jit(solution)/shard_map/dot_general | solution.py:83
  753.5 40.2 %all-reduce.4 = (f32[64,64]{1,0:T(8,128)S(1)}, f32[64,64]{0,1:T(8,128)S(1)}, f32[64,64]{1,0:T(8,128)S(1)}) all-reduce(f32[64,64]{1,0:T(8,128)S(1)} %fusion.93, f32[64,64]{0,1:T(8,128)S(1)} %fusion.92, f32[64,64]{1,0:T(8,128)S(1)} %fusion.94), channel_id=1, replica_groups=mesh['tm'=8,'panel'=4] {'tm','panel'}, use_global_device_ids=true, to_apply=%region_8.0 | all-reduce | flops 12288 | bytes 98304 | tf_op jit(solution)/shard_map/psum | solution.py:93
  809.7 63.8 %all-gather.17.cloned.1.call-done = f32[32,576,64]{1,2,0:T(8,128)} async-done(((f32[1,576,64]{1,2,0:T(8,128)}), f32[32,576,64]{1,2,0:T(8,128)}) %all-gather.17.cloned.1.call-update) | async-done | bytes 4718608 | tf_op jit(solution)/shard_map/all_gather | solution.py:85
  887.7 43.1 %fusion.96 = f32[576,64]{0,1:T(8,128)S(1)} fusion(f32[576,18432]{1,0:T(8,128)} %constant_dynamic-update-slice_fusion.2, f32[18432,64]{0,1:T(8,128)} %reshape.98), kind=kOutput, calls=%fused_computation.212 | convolution fusion | flops 8153726976 | bytes 47333376 | tf_op jit(solution)/shard_map/dot_general | solution.py:83
  932.5 40.4 %all-reduce.3 = (f32[64,64]{1,0:T(8,128)S(1)}, f32[64,64]{0,1:T(8,128)S(1)}, f32[64,64]{1,0:T(8,128)S(1)}) all-reduce(f32[64,64]{1,0:T(8,128)S(1)} %fusion.98, f32[64,64]{0,1:T(8,128)S(1)} %fusion.97, f32[64,64]{1,0:T(8,128)S(1)} %fusion.99), channel_id=1, replica_groups=mesh['tm'=8,'panel'=4] {'tm','panel'}, use_global_device_ids=true, to_apply=%region_11.0 | all-reduce | flops 12288 | bytes 98304 | tf_op jit(solution)/shard_map/psum | solution.py:93
  988.3 64.2 %all-gather.19.cloned.1.call-done = f32[32,576,64]{1,2,0:T(8,128)} async-done(((f32[1,576,64]{1,2,0:T(8,128)}), f32[32,576,64]{1,2,0:T(8,128)}) %all-gather.19.cloned.1.call-update) | async-done | bytes 4718608 | tf_op jit(solution)/shard_map/all_gather | solution.py:85
  1066.7 43.1 %fusion.101 = f32[576,64]{0,1:T(8,128)S(1)} fusion(f32[576,18432]{1,0:T(8,128)} %constant_dynamic-update-slice_fusion.2, f32[18432,64]{0,1:T(8,128)} %reshape.100), kind=kOutput, calls=%fused_computation.217 | convolution fusion | flops 8153726976 | bytes 47333376 | tf_op jit(solution)/shard_map/dot_general | solution.py:83
  1111.4 40.4 %all-reduce.2 = (f32[64,64]{1,0:T(8,128)S(1)}, f32[64,64]{0,1:T(8,128)S(1)}, f32[64,64]{1,0:T(8,128)S(1)}) all-reduce(f32[64,64]{1,0:T(8,128)S(1)} %fusion.103, f32[64,64]{0,1:T(8,128)S(1)} %fusion.102, f32[64,64]{1,0:T(8,128)S(1)} %fusion.104), channel_id=1, replica_groups=mesh['tm'=8,'panel'=4] {'tm','panel'}, use_global_device_ids=true, to_apply=%region_14.0 | all-reduce | flops 12288 | bytes 98304 | tf_op jit(solution)/shard_map/psum | solution.py:93
  1167.5 64.2 %all-gather.21.cloned.1.call-done = f32[32,576,64]{1,2,0:T(8,128)} async-done(((f32[1,576,64]{1,2,0:T(8,128)}), f32[32,576,64]{1,2,0:T(8,128)}) %all-gather.21.cloned.1.call-update) | async-done | bytes 4718608 | tf_op jit(solution)/shard_map/all_gather | solution.py:85
  1245.9 43.1 %fusion.106 = f32[576,64]{0,1:T(8,128)S(1)} fusion(f32[576,18432]{1,0:T(8,128)} %constant_dynamic-update-slice_fusion.2, f32[18432,64]{0,1:T(8,128)} %reshape.102), kind=kOutput, calls=%fused_computation.222 | convolution fusion | flops 8153726976 | bytes 47333376 | tf_op jit(solution)/shard_map/dot_general | solution.py:83
  1290.7 40.6 %all-reduce.1 = (f32[64,64]{1,0:T(8,128)S(1)}, f32[64,64]{0,1:T(8,128)S(1)}, f32[64,64]{1,0:T(8,128)S(1)}) all-reduce(f32[64,64]{1,0:T(8,128)S(1)} %fusion.108, f32[64,64]{0,1:T(8,128)S(1)} %fusion.107, f32[64,64]{1,0:T(8,128)S(1)} %fusion.109), channel_id=1, replica_groups=mesh['tm'=8,'panel'=4] {'tm','panel'}, use_global_device_ids=true, to_apply=%region_17.0 | all-reduce | flops 12288 | bytes 98304 | tf_op jit(solution)/shard_map/psum | solution.py:93
  1350.8 60.3 %all-gather.23.cloned.1.call-done = f32[32,576,64]{1,2,0:T(8,128)} async-done(((f32[1,576,64]{1,2,0:T(8,128)}), f32[32,576,64]{1,2,0:T(8,128)}) %all-gather.23.cloned.1.call-update) | async-done | bytes 4718608 | tf_op jit(solution)/shard_map/all_gather | solution.py:85
  1425.3 43.3 %fusion.111 = f32[576,64]{0,1:T(8,128)S(1)} fusion(f32[576,18432]{1,0:T(8,128)} %constant_dynamic-update-slice_fusion.2, f32[18432,64]{0,1:T(8,128)} %reshape.104), kind=kOutput, calls=%fused_computation.227 | convolution fusion | flops 8153726976 | bytes 47333376 | tf_op jit(solution)/shard_map/dot_general | solution.py:83
  1470.2 40.2 %all-reduce = (f32[64,64]{1,0:T(8,128)S(1)}, f32[64,64]{0,1:T(8,128)S(1)}, f32[64,64]{1,0:T(8,128)S(1)}) all-reduce(f32[64,64]{1,0:T(8,128)S(1)} %fusion.113, f32[64,64]{0,1:T(8,128)S(1)} %fusion.112, f32[64,64]{1,0:T(8,128)S(1)} %fusion.114), channel_id=1, replica_groups=mesh['tm'=8,'panel'=4] {'tm','panel'}, use_global_device_ids=true, to_apply=%region_20.23 | all-reduce | flops 12288 | bytes 98304 | tf_op jit(solution)/shard_map/psum | solution.py:93
  (259 shorter events, 464.5 us)
Async XLA Ops:
  8.0 99.2 %copy-start = (f32[576,64]{0,1:T(8,128)S(1)}, f32[576,64]{0,1:T(8,128)}, u32[]{:S(2)}) copy-start(f32[576,64]{0,1:T(8,128)} %param.6) | copy-start | bytes 442372
  8.0 181.1 %all-reduce.8.cloned.1.call-start = ((), (), s32[]{:S(2)}) async-start(), calls=%async_computation | async-start | bytes 7077888 | tf_op jit(solution)/shard_map/psum | solution.py:57
  8.1 3.5 collective-permute-start
  25.9 3.7 slice-start
  52.7 3.7 slice-start.1
  58.0 21.2 %collective-permute-start.1 = (f32[48,256]{1,0:T(8,128)S(1)}, f32[48,256]{1,0:T(8,128)S(1)}, u32[]{:S(2)}, u32[]{:S(2)}) collective-permute-start(f32[48,256]{1,0:T(8,128)S(1)} %collective-permute-done), channel_id=1, source_target_pairs={{4,0},{8,4},{12,8},{16,12},{20,16},{24,20},{28,24},{5,1},{9,5},{13... | collective-permute-start | bytes 147464 | tf_op jit(solution)/shard_map/ppermute | solution.py:18
  93.6 3.7 slice-start.2
  98.9 6.1 copy-start.19
  98.9 6.1 copy-start.20
  107.1 403.6 %all-gather.13.cloned.1.call-start = ((), (), s32[]{:S(2)}) async-start(), calls=%async_computation.1 | async-start | bytes 5406720 | tf_op jit(solution)/shard_map/all_gather | solution.py:85
  159.5 33.0 %copy-start.22 = (f32[64,64]{1,0:T(8,128)}, f32[64,64]{1,0:T(8,128)S(1)}, u32[]{:S(2)}) copy-start(f32[64,64]{1,0:T(8,128)S(1)} %cholesky.119) | copy-start | bytes 49156
  166.9 527.4 %all-gather.15.cloned.1.call-start = ((), (), s32[]{:S(2)}) async-start(), calls=%async_computation.2 | async-start | bytes 5406720 | tf_op jit(solution)/shard_map/all_gather | solution.py:85
  191.4 3.9 copy-start.2
  203.4 4.9 copy-start.3
  402.9 4.2 copy-start.4
  407.0 3.3 copy-start.5
  497.9 4.2 copy-start.10
  524.9 43.5 %copy-start.13 = (f32[64,576]{1,0:T(8,128)S(1)}, f32[64,576]{1,0:T(8,128)}, u32[]{:S(2)}) copy-start(f32[64,576]{1,0:T(8,128)} %get-tuple-element.51) | copy-start | bytes 442372
  524.9 43.8 %copy-start.24 = (f32[64,64]{1,0:T(8,128)S(1)}, f32[64,64]{1,0:T(8,128)}, u32[]{:S(2)}) copy-start(f32[64,64]{1,0:T(8,128)} %fusion.89) | copy-start | bytes 49156
  524.9 103.3 %copy-start.25 = (f32[7,576,64]{1,2,0:T(8,128)S(1)}, f32[7,576,64]{1,2,0:T(8,128)}, u32[]{:S(2)}) copy-start(f32[7,576,64]{1,2,0:T(8,128)} %get-tuple-element.50) | copy-start | bytes 3096580
  629.3 244.3 %all-gather.17.cloned.1.call-start = ((), (), s32[]{:S(2)}) async-start(), calls=%async_computation.3 | async-start | bytes 5406720 | tf_op jit(solution)/shard_map/all_gather | solution.py:85
  708.8 44.5 %copy-start.15 = (f32[64,576]{1,0:T(8,128)S(1)}, f32[64,576]{1,0:T(8,128)}, u32[]{:S(2)}) copy-start(f32[64,576]{1,0:T(8,128)} %get-tuple-element.53) | copy-start | bytes 442372
  808.0 244.5 %all-gather.19.cloned.1.call-start = ((), (), s32[]{:S(2)}) async-start(), calls=%async_computation.4 | async-start | bytes 5406720 | tf_op jit(solution)/shard_map/all_gather | solution.py:85
  887.7 44.5 %copy-start.16 = (f32[64,576]{1,0:T(8,128)S(1)}, f32[64,576]{1,0:T(8,128)}, u32[]{:S(2)}) copy-start(f32[64,576]{1,0:T(8,128)} %get-tuple-element.55) | copy-start | bytes 442372
  987.0 244.7 %all-gather.21.cloned.1.call-start = ((), (), s32[]{:S(2)}) async-start(), calls=%async_computation.5 | async-start | bytes 5406720 | tf_op jit(solution)/shard_map/all_gather | solution.py:85
  1066.7 44.4 %copy-start.17 = (f32[64,576]{1,0:T(8,128)S(1)}, f32[64,576]{1,0:T(8,128)}, u32[]{:S(2)}) copy-start(f32[64,576]{1,0:T(8,128)} %get-tuple-element.57) | copy-start | bytes 442372
  1166.2 245.0 %all-gather.23.cloned.1.call-start = ((), (), s32[]{:S(2)}) async-start(), calls=%async_computation.6 | async-start | bytes 5406720 | tf_op jit(solution)/shard_map/all_gather | solution.py:85
  1245.9 44.5 %copy-start.14 = (f32[64,576]{1,0:T(8,128)S(1)}, f32[64,576]{1,0:T(8,128)}, u32[]{:S(2)}) copy-start(f32[64,576]{1,0:T(8,128)} %get-tuple-element.59) | copy-start | bytes 442372
  1245.9 99.6 %copy-start.23 = (f32[64,64]{1,0:T(8,128)S(1)}, f32[64,64]{1,0:T(8,128)}, u32[]{:S(2)}) copy-start(f32[64,64]{1,0:T(8,128)} %copy-done.22) | copy-start | bytes 49156
  1425.3 44.6 %copy-start.18 = (f32[64,576]{1,0:T(8,128)S(1)}, f32[64,576]{1,0:T(8,128)}, u32[]{:S(2)}) copy-start(f32[64,576]{1,0:T(8,128)} %get-tuple-element.61) | copy-start | bytes 442372
  1425.3 101.1 %copy-start.1 = (f32[576,64]{0,1:T(8,128)S(1)}, f32[576,64]{0,1:T(8,128)}, u32[]{:S(2)}) copy-start(f32[576,64]{0,1:T(8,128)} %param.6) | copy-start | bytes 442372
  1520.2 5.3 copy-start.27
  (8 other events, 22.3 us)
Sparse Core Ops, SparseCore 0:
  107.2 81.8 all-reduce.7
Sparse Core Ops, SparseCore 1:
  167.0 69.8 all-gather.12
  629.3 65.0 all-gather.14
  808.1 65.4 all-gather.16
  987.1 65.4 all-gather.18
  1166.2 65.4 all-gather.20
  1345.6 65.4 all-gather.22
where the time goes:
time: 1550 us; the launch traced here: 1530 us
  local copies, waits for them, and re-layouts  421 us (27%)
  waiting for transfers between devices  338 us (22%)
  matrix products  309 us (20%)
  blocking collectives  294 us (19%)
  other arithmetic  139 us (9%)
  between operations  16.8 us (1%)
  starting transfers between devices  16.2 us (1%)
    all_gather x6, waiting for transfers between devices, local(): lax.all_gather(current, ('tm', 'panel'), axis=0, tiled=True)  316 us
    dot_general x6, matrix products, local(): jnp.dot(covariance, lax.all_gather(current, ('tm', 'panel'), axis=0, tile...  259 us
    psum x6, blocking collectives, local(): lax.psum((inner(current, work), inner(work, work), inner(current, current...  248 us
    reshape x12, local copies, waits for them, and re-layouts, local(): row_list.append(window.reshape(channels, M * channels))  124 us
    unnamed x85, local copies, waits for them, and re-layouts  96.2 us
    dynamic_slice x12, local copies, waits for them, and re-layouts, local(): lax.dynamic_slice(two_sided, (jnp.int32(0), M - 1 - lag_index, jnp.int32(...  93.3 us
    all_gather x6, local copies, waits for them, and re-layouts, local(): lax.all_gather(current, ('tm', 'panel'), axis=0, tiled=True)  47 us
    concatenate x2, other arithmetic, local(): jnp.concatenate([jnp.transpose(normed, (2, 1, 0))[:, :0:-1, :], normed],...  46.1 us
  transfers between devices with their start and end apart: 9, of which 7 were waited for; matrix products, arithmetic and copies ran while one was open for 23% of the time, Pallas kernels for 0%

commit v1 on v0

v1 whole, which is shorter than its diff:
```python
import jax
import jax.numpy as jnp
from jax import lax
from jax.experimental import pallas as pl
from jax.experimental.pallas import tpu as pltpu
from jax.sharding import PartitionSpec as P

M = 384
ITERS = 6
GROUP = 16
K_STEP = 1280
CHUNK = 1536

exact_precision = lax.Precision.HIGHEST
f32 = jnp.float32
bf16 = jnp.bfloat16


def shifted_around(block, axis):
    size = lax.axis_size(axis)
    received = [block]
    for distance in range(1, size):
        route = [(i, (i + distance) % size) for i in range(size)]
        received.append(lax.ppermute(block, axis, route))
    return received


def exact_dot(left, right, dims=((1,), (0,))):
    return lax.dot_general(
        left, right, (dims, ((), ())), precision=exact_precision, preferred_element_type=f32
    )


def fast_dot(left, right):
    return jnp.dot(left, right, preferred_element_type=f32)


def lag_kernel(both_ref, high_ref, low_ref, count_ref, window_ref, split_ref):
    channels = both_ref.shape[0] // 2
    days = both_ref.shape[1]
    width = high_ref.shape[1]
    day_step = min(days, 2048)

    def group(g, carry):
        total = jnp.zeros((channels, width), f32)
        for first in range(0, days, day_step):
            row = pl.multiple_of(g * GROUP + first, GROUP)
            left = both_ref[:, first : first + day_step]
            high = fast_dot(left, high_ref[pl.ds(row, day_step), :])
            low = fast_dot(left[:channels], low_ref[pl.ds(row, day_step), :])
            total = total + (high[:channels] + (high[channels:] + low))
        lanes = pl.ds(pl.multiple_of(g * width, 128), width)
        value = total / count_ref[:, lanes]
        window_ref[:, lanes] = value
        upper_half = value.astype(bf16)
        split_ref[:channels, lanes] = upper_half
        split_ref[channels:, lanes] = (value - upper_half.astype(f32)).astype(bf16)
        return carry

    lax.fori_loop(0, window_ref.shape[1] // width, group, 0)


def split_halves(values):
    high = lax.reduce_precision(values, 8, 7)
    return high.astype(bf16), (values - high).astype(bf16)


def lag_window(series, block_index, lags_here):
    channels, days = series.shape
    groups = -(-(M + lags_here) // GROUP)
    rows = days + groups * GROUP
    width = GROUP * channels
    padded = jnp.pad(series.T, ((M, rows + GROUP - days), (0, 0)))
    base = M - (lags_here - 1) - block_index * lags_here
    placed = lax.dynamic_slice(padded, (base, jnp.int32(0)), (rows + GROUP, channels))
    high, low = split_halves(placed)
    high = jnp.concatenate([high[r : r + rows] for r in range(GROUP)], axis=1)
    low = jnp.concatenate([low[r : r + rows] for r in range(GROUP)], axis=1)
    both = jnp.concatenate(split_halves(series), axis=0)
    lag = jnp.arange(groups * GROUP) - (lags_here - 1) - block_index * lags_here
    count = jnp.repeat((days - jnp.abs(lag)).astype(f32), channels)[None, :]
    length = groups * width
    return pl.pallas_call(
        lag_kernel,
        out_shape=(
            jax.ShapeDtypeStruct((channels, length), f32),
            jax.ShapeDtypeStruct((2 * channels, length), bf16),
        ),
        name="lag_window",
    )(both, high, low, count)


def covariance_kernel(window_ref, out_ref):
    channels, length = out_ref.shape
    lags_here = pl.num_programs(0)
    for shift in range(M):
        if shift >= covariance_kernel.lags:
            break

        @pl.when(pl.program_id(0) == lags_here - 1 - shift)
        def _(shift=shift):
            first = shift * channels
            aligned = first // 128 * 128
            rest = first - aligned

            def chunk(c, carry):
                source = pl.multiple_of(aligned + c * CHUNK, 128)
                piece = window_ref[:, pl.ds(source, CHUNK + 128)]
                out_ref[:, pl.ds(pl.multiple_of(c * CHUNK, 128), CHUNK)] = piece[:, rest : rest + CHUNK]
                return carry

            lax.fori_loop(0, length // CHUNK, chunk, 0)


def covariance_rows(window, lags_here):
    channels = window.shape[0]
    length = M * channels
    covariance_kernel.lags = lags_here
    return pl.pallas_call(
        covariance_kernel,
        grid=(lags_here,),
        in_specs=[pl.BlockSpec(window.shape, lambda i: (0, 0))],
        out_specs=pl.BlockSpec((channels, length), lambda i: (i, 0)),
        out_shape=jax.ShapeDtypeStruct((lags_here * channels, length), f32),
        name="covariance_rows",
    )(window)


def factor_and_inverse(gram, result_ref):
    n = gram.shape[0]
    row_id = lax.broadcasted_iota(jnp.int32, (n, n), 0)
    col_id = lax.broadcasted_iota(jnp.int32, (n, n), 1)
    rest = jnp.concatenate([gram, (row_id == col_id).astype(f32)], axis=1)
    for k in range(n):
        at = k % 8
        if k and at == 0:
            rest = rest[8:]
        row = rest[at : at + 1]
        pivot = row[:, k : k + 1]
        root = lax.rsqrt(pivot)
        root = root * (1.5 - 0.5 * pivot * root * root)
        row = row * root
        result_ref[k : k + 1, :] = row
        below = lax.broadcasted_iota(jnp.int32, (rest.shape[0], 1), 0) > at
        column = jnp.where(below, rest[:, k : k + 1] * root, 0.0)
        rest = rest - column * row
    upper = jnp.where(col_id >= row_id, result_ref[:, :n], 0.0)
    return upper, result_ref[:, n:]


def orthogonalize(gram, work, current, result_ref):
    n = work.shape[1]
    diagonal = gram[:n, n:]
    weighted = exact_dot(gram[:n, :n], diagonal) - 2.0 * diagonal
    reduced = gram[n:, n:] + exact_dot(diagonal, weighted, ((0,), (0,)))
    upper, inverse = factor_and_inverse(reduced, result_ref)
    cleaned = work - exact_dot(current, diagonal)
    return diagonal, upper, inverse, exact_dot(cleaned, inverse, ((1,), (1,)))


def step_kernel(place_ref, *refs):
    tm_size = step_kernel.tm_size
    panel_size = step_kernel.panel_size
    received = refs[:tm_size]
    split_ref, work_ref, current_ref, product_ref = refs[tm_size : tm_size + 4]
    next_ref, next_product_ref, next_work_ref, packed_ref, gram_ref, diagonal_ref, upper_ref = refs[
        tm_size + 4 : tm_size + 11
    ]
    pairs_ref, high_ref, low_ref, total_ref, result_ref = refs[tm_size + 11 :]
    rows, n = work_ref.shape
    half = rows // 2
    channels = split_ref.shape[0] // 2
    lags_here = rows // channels
    pair_count = (lags_here + 1) // 2
    front = 2 * pair_count * channels
    length = split_ref.shape[1]
    data = tm_size * panel_size * rows

    pairs_ref[: front + channels, :] = jnp.zeros((front + channels, 2 * n), f32)
    tail = pairs_ref.shape[0] - (front + data)
    pairs_ref[front + data :, :] = jnp.zeros((tail, 2 * n), f32)
    for step in range(tm_size):
        origin = lax.rem(place_ref[0] + tm_size - step, tm_size) * panel_size

        def unpack(p, carry, step=step, origin=origin):
            source = lax.rem(place_ref[1] + panel_size - p, panel_size)
            to = pl.multiple_of(front + (origin + source) * rows, 8)
            value = received[step][pl.ds(pl.multiple_of(p * half, 8), half), :]
            swapped = pltpu.roll(value, n, 1)
            pairs_ref[pl.ds(to, half), :n] = value[:, :n]
            pairs_ref[pl.ds(to + half, half), :n] = swapped[:, :n]
            pairs_ref[pl.ds(to + channels, half), n:] = swapped[:, n:]
            pairs_ref[pl.ds(to + channels + half, half), n:] = value[:, n:]
            return carry

        lax.fori_loop(0, panel_size, unpack, 0)

    def halves(c, carry):
        at = pl.ds(pl.multiple_of(c * 96, 32), 96)
        value = pairs_ref[at, :]
        upper_half = value.astype(bf16)
        high_ref[at, :] = upper_half
        low_ref[at, :] = (value - upper_half.astype(f32)).astype(bf16)
        return carry

    lax.fori_loop(0, pairs_ref.shape[0] // 96, halves, 0)

    total_ref[...] = jnp.zeros(total_ref.shape, f32)

    def multiply(c, carry):
        first = c * K_STEP
        left = split_ref[:, pl.ds(pl.multiple_of(first, 128), K_STEP)]
        for pair in range(0, pair_count, 2):
            group = range(pair, min(pair + 2, pair_count))
            at = [pl.ds(pl.multiple_of(first + front - 2 * channels * j, 16), K_STEP) for j in group]
            high = jnp.concatenate([high_ref[s, :] for s in at], axis=1)
            low = jnp.concatenate([low_ref[s, :] for s in at], axis=1)
            lanes = slice(pair * 2 * n, (pair + len(group)) * 2 * n)
            first_part = fast_dot(left, high)
            second_part = fast_dot(left[:channels], low)
            total_ref[:, lanes] += first_part[:channels] + (first_part[channels:] + second_part)
        return carry

    lax.fori_loop(0, length // K_STEP, multiply, 0)
    for shift in range(lags_here):
        at = (lags_here - 1 - shift) * channels
        next_product_ref[at : at + channels, :] = total_ref[:, shift * n : (shift + 1) * n]

    gram = received[0][panel_size * half :, :]
    for step in range(1, tm_size):
        gram = gram + received[step][panel_size * half :, :]
    current = current_ref[...]
    diagonal, upper, inverse, following = orthogonalize(gram, work_ref[...], current, result_ref)
    product = next_product_ref[...] - exact_dot(product_ref[...], diagonal)
    product = exact_dot(product, inverse, ((1,), (1,)))
    work = product - exact_dot(current, upper, ((1,), (1,)))
    diagonal_ref[...] = diagonal
    upper_ref[...] = upper
    next_ref[...] = following
    next_product_ref[...] = product
    next_work_ref[...] = work
    packed_ref[:, :n] = work[:half]
    packed_ref[:, n:] = work[half:]
    together = jnp.concatenate([following, work], axis=1)
    gram_ref[...] = exact_dot(together, together, ((0,), (0,)))


def last_kernel(*refs):
    received = refs[:-7]
    work_ref, current_ref, next_ref, diagonal_ref, upper_ref, result_ref = refs[-6:]
    gram = refs[-7][...]
    for other in received:
        gram = gram + other[...]
    diagonal, upper, _, following = orthogonalize(gram, work_ref[...], current_ref[...], result_ref)
    diagonal_ref[...] = diagonal
    upper_ref[...] = upper
    next_ref[...] = following


def lanczos_step(place, received, split, work, current, product):
    rows, n = work.shape
    channels = split.shape[0] // 2
    pair_count = (rows // channels + 1) // 2
    front = 2 * pair_count * channels
    depth = front + split.shape[1] + 2 * channels
    depth = -(-depth // 96) * 96
    step_kernel.tm_size = lax.axis_size("tm")
    step_kernel.panel_size = lax.axis_size("panel")
    tall = jax.ShapeDtypeStruct((rows, n), f32)
    small = jax.ShapeDtypeStruct((n, n), f32)
    vmem = pl.BlockSpec(memory_space=pltpu.VMEM)
    return pl.pallas_call(
        step_kernel,
        in_specs=[pl.BlockSpec(memory_space=pltpu.SMEM)] + [vmem] * (len(received) + 4),
        out_shape=(
            tall,
            tall,
            tall,
            jax.ShapeDtypeStruct((rows // 2, 2 * n), f32),
            jax.ShapeDtypeStruct((2 * n, 2 * n), f32),
            small,
            small,
        ),
        scratch_shapes=[
            pltpu.VMEM((depth, 2 * n), f32),
            pltpu.VMEM((depth, 2 * n), bf16),
            pltpu.VMEM((depth, 2 * n), bf16),
            pltpu.VMEM((channels, pair_count * 2 * n), f32),
            pltpu.VMEM((n, 2 * n), f32),
        ],
        name="lanczos_step",
    )(place, *received, split, work, current, product)


def last_step(received, work, current):
    n = work.shape[1]
    small = jax.ShapeDtypeStruct((n, n), f32)
    return pl.pallas_call(
        last_kernel,
        out_shape=(jax.ShapeDtypeStruct(work.shape, f32), small, small),
        scratch_shapes=[pltpu.VMEM((n, 2 * n), f32)],
        name="last_step",
    )(*received, work, current)


def exchanged(packed, gram):
    half = packed.shape[0]
    near = shifted_around(jnp.concatenate([packed, gram], axis=0), "panel")
    gram = sum(piece[half:] for piece in near[1:]) + near[0][half:]
    group = jnp.concatenate([piece[:half] for piece in near] + [gram], axis=0)
    return shifted_around(group, "tm")


def local(series, start_block):
    channels, days_here = series.shape
    rows, n = start_block.shape
    tm_size = lax.axis_size("tm")
    tm_at = lax.axis_index("tm")
    panel_at = lax.axis_index("panel")
    lags_here = rows // channels
    block_index = tm_at * lax.axis_size("panel") + panel_at

    packed = jnp.concatenate([start_block[: rows // 2], start_block[rows // 2 :]], axis=1)
    start_gram = exact_dot(start_block, start_block, ((0,), (0,)))
    gram = jnp.pad(start_gram, ((n, 0), (n, 0)))

    pieces = shifted_around(series, "tm")
    twice = jnp.concatenate(pieces[::-1] + pieces[::-1], axis=1)
    first = (tm_size - 1 - tm_at) * days_here
    whole = lax.dynamic_slice(twice, (jnp.int32(0), first), (channels, tm_size * days_here))
    window, split = lag_window(whole, block_index, lags_here)
    covariance = covariance_rows(window, lags_here)

    place = jnp.stack([tm_at, panel_at]).astype(jnp.int32)
    work = start_block
    current = jnp.zeros_like(work)
    product = jnp.zeros_like(work)
    basis_list, diagonal_list, upper_list = [], [], []
    for _ in range(ITERS):
        received = exchanged(packed, gram)
        current, product, work, packed, gram, diagonal, upper = lanczos_step(
            place, received, split, work, current, product
        )
        basis_list.append(current)
        diagonal_list.append(diagonal)
        upper_list.append(upper)
    near = shifted_around(gram, "panel")
    grams = shifted_around(sum(near[1:]) + near[0], "tm")
    current, diagonal, upper = last_step(grams, work, current)
    basis_list.append(current)
    diagonal_list.append(diagonal)
    upper_list.append(upper)
    return (
        covariance,
        jnp.stack(basis_list),
        jnp.stack(diagonal_list[1:]),
        jnp.stack(upper_list),
    )


def solution(mesh):
    placed = (P(None, "tm"), P(("tm", "panel"), None))
    return jax.shard_map(
        local,
        mesh=mesh,
        in_specs=placed,
        out_specs=(P(("tm", "panel"), None), P(None, ("tm", "panel"), None), P(), P()),
        check_vma=False,
    )
```

time: 1550 us -> 790 us (0.51)
  local copies, waits for them, and re-layouts: 421 us -> 66.2 us
  matrix products: 309 us -> 1.29 us
  blocking collectives: 294 us -> 0 us
  Pallas kernels: 0 us -> 241 us
  other arithmetic: 139 us -> 7.32 us
  starting transfers between devices: 16.2 us -> 73 us
  waiting for transfers between devices: 338 us -> 392 us
    ppermute x2 -> x77, waiting for transfers between devices: 1.23 us -> 392 us  [shifted_around(): received.append(lax.ppermute(block, axis, route))]
    all_gather x6 -> x0, waiting for transfers between devices: 316 us -> none  [local(): lax.all_gather(current, ('tm', 'panel'), axis=0, tiled=True)]
    dot_general x57 -> x1, matrix products: 302 us -> 1.29 us  [exact_dot(): lax.dot_general(left, right, (dims, ((), ())), precision=exact_precision,...]
    psum x7 -> x0, blocking collectives: 294 us -> none  [the longest x6 248 us: local(): lax.psum((inner(current, work), inner(work, work), inner(current, current...]
    pallas_call x0 -> x8, Pallas kernels: none -> 241 us  [the longest x6 181 us: lanczos_step(): pl.pallas_call(step_kernel, in_specs=[pl.BlockSpec(memory_space=pltpu.SME...]
    reshape x12 -> x0, local copies, waits for them, and re-layouts: 124 us -> none  [local(): row_list.append(window.reshape(channels, M * channels))]
    dynamic_slice x12 -> x1, local copies, waits for them, and re-layouts: 93.3 us -> 0.04 us  [local(): lax.dynamic_slice(twice, (jnp.int32(0), first), (channels, tm_size * days...]
    another operation x36 -> x1, other arithmetic: 85.2 us -> 0.61 us  [local(): place = jnp.stack([tm_at, panel_at]).astype(jnp.int32)]
  transfers between devices with their start and end apart: 9 -> 77, of which waited for: 7 -> 43; matrix products, arithmetic and copies ran while one was open for 23% -> 5% of each run, Pallas kernels for 0% -> 8%
where the time goes in v1:
time: 790 us; the launch traced here: 784 us
  waiting for transfers between devices  392 us (50%)
  Pallas kernels  241 us (31%)
  starting transfers between devices  73 us (9%)
  local copies, waits for them, and re-layouts  66.2 us (8%)
    ppermute x77, waiting for transfers between devices, shifted_around(): received.append(lax.ppermute(block, axis, route))  392 us
    pallas_call x6, Pallas kernels, lanczos_step(): pl.pallas_call(step_kernel, in_specs=[pl.BlockSpec(memory_space=pltpu.SME...  181 us
    ppermute x77, starting transfers between devices, shifted_around(): received.append(lax.ppermute(block, axis, route))  73 us
    pallas_call x1, Pallas kernels, lag_window(): pl.pallas_call(lag_kernel, out_shape=(jax.ShapeDtypeStruct((channels, len...  35.3 us
    pallas_call x1, Pallas kernels, covariance_rows(): pl.pallas_call(covariance_kernel, grid=(lags_here,), in_specs=[pl.BlockSp...  25.4 us
    unnamed x175, local copies, waits for them, and re-layouts  22.3 us
  transfers between devices with their start and end apart: 77, of which 43 were waited for; matrix products, arithmetic and copies ran while one was open for 5% of the time, Pallas kernels for 8%

profile of v1, /device:TPU:0, one launch (start us, length us, event | category | flops | bytes accessed | tf_op | source)
XLA Modules:
  0.0 783.5 jit_solution(7347891224769517098)
XLA Ops:
  23.8 10.7 %collective-permute-done.7 = f32[416,128]{1,0:T(8,128)S(1)} collective-permute-done((f32[416,128]{1,0:T(8,128)S(1)}, f32[416,128]{1,0:T(8,128)S(1)}, u32[]{:S(2)}, u32[]{:S(2)}) %collective-permute-start.7) | collective-permute-done | bytes 213024 | tf_op jit(solution)/shard_map/ppermute | solution.py:24
  47.0 10.9 %concatenate.54.low_ref = bf16[2448,768]{1,0:T(8,128)(2,1)} concatenate(bf16[2448,48]{1,0:T(8,128)(2,1)} %get-tuple-element.129, bf16[2448,48]{1,0:T(8,128)(2,1)} %get-tuple-element.128, bf16[2448,48]{1,0:T(8,128)(2,1)} %get-tuple-element.127, bf16[2448,48]{1,0:T(8,128)(2,1)} %get-tuple-element.126, bf16[2448,48]{1,0:T(8,128)(2,1)} %get-tuple-element.125, ...), dimensions={1} | concatenate | bytes 7520256 | tf_op jit(solution)/shard_map/concatenate | solution.py:78
  62.1 9.0 %collective-permute-done.15.refs_6_ = f32[1280,128]{1,0:T(8,128)} collective-permute-done((f32[1280,128]{1,0:T(8,128)}, f32[1280,128]{1,0:T(8,128)}, u32[]{:S(2)}, u32[]{:S(2)}) %collective-permute-start.15) | collective-permute-done | bytes 655392 | tf_op jit(solution)/shard_map/ppermute | solution.py:24
  75.3 10.9 %concatenate.53.high_ref = bf16[2448,768]{1,0:T(8,128)(2,1)} concatenate(bf16[2448,48]{1,0:T(8,128)(2,1)} %get-tuple-element.145, bf16[2448,48]{1,0:T(8,128)(2,1)} %get-tuple-element.144, bf16[2448,48]{1,0:T(8,128)(2,1)} %get-tuple-element.143, bf16[2448,48]{1,0:T(8,128)(2,1)} %get-tuple-element.142, bf16[2448,48]{1,0:T(8,128)(2,1)} %get-tuple-element.141, ...), dimensions={1} | concatenate | bytes 7520256 | tf_op jit(solution)/shard_map/concatenate | solution.py:77
  86.1 35.3 %lag_window.1 = (f32[48,19200]{1,0:T(8,128)}, bf16[96,19200]{1,0:T(8,128)(2,1)}) custom-call(bf16[96,2048]{1,0:T(8,128)(2,1)} %copy.35.both_ref, bf16[2448,768]{1,0:T(8,128)(2,1)} %concatenate.53.high_ref, bf16[2448,768]{1,0:T(8,128)(2,1)} %concatenate.54.low_ref, f32[1,19200]{1,0:T(1,128)} %broadcast_in_dim_reshape.3.count_ref), custom_call_target="tpu_custom_call" | custom-call | tf_op jit(solution)/shard_map/lag_window/pallas_call | solution.py:83
  122.2 30.1 %lanczos_step.6 = (f32[576,64]{1,0:T(8,128)}, f32[576,64]{1,0:T(8,128)}, f32[576,64]{1,0:T(8,128)}, f32[288,128]{1,0:T(8,128)}, f32[128,128]{1,0:T(8,128)}, /*index=5*/f32[64,64]{1,0:T(8,128)}, f32[64,64]{1,0:T(8,128)}) custom-call(s32[2]{0:T(128)} %pad_add_fusion.place_ref, f32[1280,128]{1,0:T(8,128)} %constant_dynamic-update-slice_fusion.16.refs_0_, ...), custom_call_target="tpu_custom_call" | custom-call | tf_op jit(solution)/shard_map/lanczos_step/pallas_call | solution.py:272
  164.1 13.3 %collective-permute-done.18 = f32[416,128]{1,0:T(8,128)S(1)} collective-permute-done((f32[416,128]{1,0:T(8,128)S(1)}, f32[416,128]{1,0:T(8,128)S(1)}, u32[]{:S(2)}, u32[]{:S(2)}) %collective-permute-start.18) | collective-permute-done | bytes 213024 | tf_op jit(solution)/shard_map/ppermute | solution.py:24
  183.0 12.4 %collective-permute-done.26.refs_7_ = f32[1280,128]{1,0:T(8,128)S(1)} collective-permute-done((f32[1280,128]{1,0:T(8,128)S(1)}, f32[1280,128]{1,0:T(8,128)S(1)}, u32[]{:S(2)}, u32[]{:S(2)}) %collective-permute-start.26) | collective-permute-done | bytes 655392 | tf_op jit(solution)/shard_map/ppermute | solution.py:24
  195.5 14.3 %collective-permute-done.25.refs_6_ = f32[1280,128]{1,0:T(8,128)S(1)} collective-permute-done((f32[1280,128]{1,0:T(8,128)S(1)}, f32[1280,128]{1,0:T(8,128)S(1)}, u32[]{:S(2)}, u32[]{:S(2)}) %collective-permute-start.25) | collective-permute-done | bytes 655392 | tf_op jit(solution)/shard_map/ppermute | solution.py:24
  209.9 29.6 %collective-permute-done.23.refs_4_ = f32[1280,128]{1,0:T(8,128)S(1)} collective-permute-done((f32[1280,128]{1,0:T(8,128)S(1)}, f32[1280,128]{1,0:T(8,128)S(1)}, u32[]{:S(2)}, u32[]{:S(2)}) %collective-permute-start.23) | collective-permute-done | bytes 655392 | tf_op jit(solution)/shard_map/ppermute | solution.py:24
  242.0 30.1 %lanczos_step.7 = (f32[576,64]{1,0:T(8,128)}, f32[576,64]{1,0:T(8,128)}, f32[576,64]{1,0:T(8,128)}, f32[288,128]{1,0:T(8,128)}, f32[128,128]{1,0:T(8,128)}, /*index=5*/f32[64,64]{1,0:T(8,128)}, f32[64,64]{1,0:T(8,128)}) custom-call(s32[2]{0:T(128)} %pad_add_fusion.place_ref, f32[1280,128]{1,0:T(8,128)} %copy-done.8, f32[1280,128]{1,0:T(8,128)} %copy-done.43, ...), custom_call_target="tpu_custom_call" | custom-call | tf_op jit(solution)/shard_map/lanczos_step/pallas_call | solution.py:272
  283.9 9.9 %collective-permute-done.28 = f32[416,128]{1,0:T(8,128)S(1)} collective-permute-done((f32[416,128]{1,0:T(8,128)S(1)}, f32[416,128]{1,0:T(8,128)S(1)}, u32[]{:S(2)}, u32[]{:S(2)}) %collective-permute-start.28) | collective-permute-done | bytes 213024 | tf_op jit(solution)/shard_map/ppermute | solution.py:24
  298.8 11.2 %collective-permute-done.36.refs_7_ = f32[1280,128]{1,0:T(8,128)S(1)} collective-permute-done((f32[1280,128]{1,0:T(8,128)S(1)}, f32[1280,128]{1,0:T(8,128)S(1)}, u32[]{:S(2)}, u32[]{:S(2)}) %collective-permute-start.36) | collective-permute-done | bytes 655392 | tf_op jit(solution)/shard_map/ppermute | solution.py:24
  310.5 14.5 %collective-permute-done.35.refs_6_ = f32[1280,128]{1,0:T(8,128)S(1)} collective-permute-done((f32[1280,128]{1,0:T(8,128)S(1)}, f32[1280,128]{1,0:T(8,128)S(1)}, u32[]{:S(2)}, u32[]{:S(2)}) %collective-permute-start.35) | collective-permute-done | bytes 655392 | tf_op jit(solution)/shard_map/ppermute | solution.py:24
  326.0 27.9 %collective-permute-done.33.refs_4_ = f32[1280,128]{1,0:T(8,128)S(1)} collective-permute-done((f32[1280,128]{1,0:T(8,128)S(1)}, f32[1280,128]{1,0:T(8,128)S(1)}, u32[]{:S(2)}, u32[]{:S(2)}) %collective-permute-start.33) | collective-permute-done | bytes 655392 | tf_op jit(solution)/shard_map/ppermute | solution.py:24
  356.8 30.1 %lanczos_step.8 = (f32[576,64]{1,0:T(8,128)}, f32[576,64]{1,0:T(8,128)}, f32[576,64]{1,0:T(8,128)}, f32[288,128]{1,0:T(8,128)}, f32[128,128]{1,0:T(8,128)}, /*index=5*/f32[64,64]{1,0:T(8,128)}, f32[64,64]{1,0:T(8,128)}) custom-call(s32[2]{0:T(128)} %pad_add_fusion.place_ref, f32[1280,128]{1,0:T(8,128)} %copy-done.9, f32[1280,128]{1,0:T(8,128)} %copy-done.44, ...), custom_call_target="tpu_custom_call" | custom-call | tf_op jit(solution)/shard_map/lanczos_step/pallas_call | solution.py:272
  398.7 8.7 %collective-permute-done.38 = f32[416,128]{1,0:T(8,128)S(1)} collective-permute-done((f32[416,128]{1,0:T(8,128)S(1)}, f32[416,128]{1,0:T(8,128)S(1)}, u32[]{:S(2)}, u32[]{:S(2)}) %collective-permute-start.38) | collective-permute-done | bytes 213024 | tf_op jit(solution)/shard_map/ppermute | solution.py:24
  411.6 11.8 %collective-permute-done.46.refs_7_ = f32[1280,128]{1,0:T(8,128)S(1)} collective-permute-done((f32[1280,128]{1,0:T(8,128)S(1)}, f32[1280,128]{1,0:T(8,128)S(1)}, u32[]{:S(2)}, u32[]{:S(2)}) %collective-permute-start.46) | collective-permute-done | bytes 655392 | tf_op jit(solution)/shard_map/ppermute | solution.py:24
  423.4 14.0 %collective-permute-done.45.refs_6_ = f32[1280,128]{1,0:T(8,128)S(1)} collective-permute-done((f32[1280,128]{1,0:T(8,128)S(1)}, f32[1280,128]{1,0:T(8,128)S(1)}, u32[]{:S(2)}, u32[]{:S(2)}) %collective-permute-start.45) | collective-permute-done | bytes 655392 | tf_op jit(solution)/shard_map/ppermute | solution.py:24
  439.5 27.6 %collective-permute-done.43.refs_4_ = f32[1280,128]{1,0:T(8,128)S(1)} collective-permute-done((f32[1280,128]{1,0:T(8,128)S(1)}, f32[1280,128]{1,0:T(8,128)S(1)}, u32[]{:S(2)}, u32[]{:S(2)}) %collective-permute-start.43) | collective-permute-done | bytes 655392 | tf_op jit(solution)/shard_map/ppermute | solution.py:24
  470.3 30.1 %lanczos_step.9 = (f32[576,64]{1,0:T(8,128)}, f32[576,64]{1,0:T(8,128)}, f32[576,64]{1,0:T(8,128)}, f32[288,128]{1,0:T(8,128)}, f32[128,128]{1,0:T(8,128)}, /*index=5*/f32[64,64]{1,0:T(8,128)}, f32[64,64]{1,0:T(8,128)}) custom-call(s32[2]{0:T(128)} %pad_add_fusion.place_ref, f32[1280,128]{1,0:T(8,128)} %copy-done.10, f32[1280,128]{1,0:T(8,128)} %copy-done.45, ...), custom_call_target="tpu_custom_call" | custom-call | tf_op jit(solution)/shard_map/lanczos_step/pallas_call | solution.py:272
  502.2 25.4 %covariance_rows.1 = f32[576,18432]{1,0:T(8,128)} custom-call(f32[48,19200]{1,0:T(8,128)} %get-tuple-element.48.window_ref), custom_call_target="tpu_custom_call" | custom-call | tf_op jit(solution)/shard_map/covariance_rows/pallas_call | solution.py:119
  531.5 10.8 %collective-permute-done.48 = f32[416,128]{1,0:T(8,128)S(1)} collective-permute-done((f32[416,128]{1,0:T(8,128)S(1)}, f32[416,128]{1,0:T(8,128)S(1)}, u32[]{:S(2)}, u32[]{:S(2)}) %collective-permute-start.48) | collective-permute-done | bytes 213024 | tf_op jit(solution)/shard_map/ppermute | solution.py:24
  546.0 11.5 %collective-permute-done.56.refs_7_ = f32[1280,128]{1,0:T(8,128)S(1)} collective-permute-done((f32[1280,128]{1,0:T(8,128)S(1)}, f32[1280,128]{1,0:T(8,128)S(1)}, u32[]{:S(2)}, u32[]{:S(2)}) %collective-permute-start.56) | collective-permute-done | bytes 655392 | tf_op jit(solution)/shard_map/ppermute | solution.py:24
  557.4 14.0 %collective-permute-done.55.refs_6_ = f32[1280,128]{1,0:T(8,128)S(1)} collective-permute-done((f32[1280,128]{1,0:T(8,128)S(1)}, f32[1280,128]{1,0:T(8,128)S(1)}, u32[]{:S(2)}, u32[]{:S(2)}) %collective-permute-start.55) | collective-permute-done | bytes 655392 | tf_op jit(solution)/shard_map/ppermute | solution.py:24
  573.7 28.0 %collective-permute-done.53.refs_4_ = f32[1280,128]{1,0:T(8,128)S(1)} collective-permute-done((f32[1280,128]{1,0:T(8,128)S(1)}, f32[1280,128]{1,0:T(8,128)S(1)}, u32[]{:S(2)}, u32[]{:S(2)}) %collective-permute-start.53) | collective-permute-done | bytes 655392 | tf_op jit(solution)/shard_map/ppermute | solution.py:24
  604.2 30.2 %lanczos_step.10 = (f32[576,64]{1,0:T(8,128)}, f32[576,64]{1,0:T(8,128)}, f32[576,64]{1,0:T(8,128)}, f32[288,128]{1,0:T(8,128)}, f32[128,128]{1,0:T(8,128)}, /*index=5*/f32[64,64]{1,0:T(8,128)}, f32[64,64]{1,0:T(8,128)}) custom-call(s32[2]{0:T(128)} %pad_add_fusion.place_ref, f32[1280,128]{1,0:T(8,128)} %copy-done.7, f32[1280,128]{1,0:T(8,128)} %copy-done.35, ...), custom_call_target="tpu_custom_call" | custom-call | tf_op jit(solution)/shard_map/lanczos_step/pallas_call | solution.py:272
  647.1 11.5 %collective-permute-done.58 = f32[416,128]{1,0:T(8,128)S(1)} collective-permute-done((f32[416,128]{1,0:T(8,128)S(1)}, f32[416,128]{1,0:T(8,128)S(1)}, u32[]{:S(2)}, u32[]{:S(2)}) %collective-permute-start.58) | collective-permute-done | bytes 213024 | tf_op jit(solution)/shard_map/ppermute | solution.py:24
  664.4 10.0 %collective-permute-done.66.refs_7_ = f32[1280,128]{1,0:T(8,128)S(1)} collective-permute-done((f32[1280,128]{1,0:T(8,128)S(1)}, f32[1280,128]{1,0:T(8,128)S(1)}, u32[]{:S(2)}, u32[]{:S(2)}) %collective-permute-start.66) | collective-permute-done | bytes 655392 | tf_op jit(solution)/shard_map/ppermute | solution.py:24
  676.0 14.5 %collective-permute-done.65.refs_6_ = f32[1280,128]{1,0:T(8,128)S(1)} collective-permute-done((f32[1280,128]{1,0:T(8,128)S(1)}, f32[1280,128]{1,0:T(8,128)S(1)}, u32[]{:S(2)}, u32[]{:S(2)}) %collective-permute-start.65) | collective-permute-done | bytes 655392 | tf_op jit(solution)/shard_map/ppermute | solution.py:24
  691.0 28.8 %collective-permute-done.63.refs_4_ = f32[1280,128]{1,0:T(8,128)S(1)} collective-permute-done((f32[1280,128]{1,0:T(8,128)S(1)}, f32[1280,128]{1,0:T(8,128)S(1)}, u32[]{:S(2)}, u32[]{:S(2)}) %collective-permute-start.63) | collective-permute-done | bytes 655392 | tf_op jit(solution)/shard_map/ppermute | solution.py:24
  722.0 30.1 %lanczos_step.11 = (f32[576,64]{1,0:T(8,128)}, f32[576,64]{1,0:T(8,128)}, f32[576,64]{1,0:T(8,128)}, f32[288,128]{1,0:T(8,128)}, f32[128,128]{1,0:T(8,128)}, /*index=5*/f32[64,64]{1,0:T(8,128)}, f32[64,64]{1,0:T(8,128)}) custom-call(s32[2]{0:T(128)} %pad_add_fusion.place_ref, f32[1280,128]{1,0:T(8,128)} %copy-done.6, f32[1280,128]{1,0:T(8,128)} %copy-done.39, ...), custom_call_target="tpu_custom_call" | custom-call | tf_op jit(solution)/shard_map/lanczos_step/pallas_call | solution.py:272
  (340 shorter events, 174.0 us)
Async XLA Ops:
  57.9 63.5 %collective-permute-start.14 = (f32[1280,128]{1,0:T(8,128)}, f32[1280,128]{1,0:T(8,128)}, u32[]{:S(2)}, u32[]{:S(2)}) collective-permute-start(f32[1280,128]{1,0:T(8,128)} %constant_dynamic-update-slice_fusion.16.refs_0_), channel_id=1, source_target_pairs={{0,20},{4,24},{8,28},{12,0},{16,4},{20,8},{24,12},{28,16},{1,21},{... | collective-permute-start | bytes 1966088 | tf_op jit(solution)/shard_map/ppermute | solution.py:24
  58.7 62.7 %collective-permute-start.13 = (f32[1280,128]{1,0:T(8,128)}, f32[1280,128]{1,0:T(8,128)}, u32[]{:S(2)}, u32[]{:S(2)}) collective-permute-start(f32[1280,128]{1,0:T(8,128)} %constant_dynamic-update-slice_fusion.16.refs_0_), channel_id=1, source_target_pairs={{0,16},{4,20},{8,24},{12,28},{16,0},{20,4},{24,8},{28,12},{1,17},{... | collective-permute-start | bytes 1966088 | tf_op jit(solution)/shard_map/ppermute | solution.py:24
  59.8 61.6 %collective-permute-start.12 = (f32[1280,128]{1,0:T(8,128)}, f32[1280,128]{1,0:T(8,128)}, u32[]{:S(2)}, u32[]{:S(2)}) collective-permute-start(f32[1280,128]{1,0:T(8,128)} %constant_dynamic-update-slice_fusion.16.refs_0_), channel_id=1, source_target_pairs={{0,12},{4,16},{8,20},{12,24},{16,28},{20,0},{24,4},{28,8},{1,13},{... | collective-permute-start | bytes 1966088 | tf_op jit(solution)/shard_map/ppermute | solution.py:24
  60.3 61.1 %collective-permute-start.11 = (f32[1280,128]{1,0:T(8,128)}, f32[1280,128]{1,0:T(8,128)}, u32[]{:S(2)}, u32[]{:S(2)}) collective-permute-start(f32[1280,128]{1,0:T(8,128)} %constant_dynamic-update-slice_fusion.16.refs_0_), channel_id=1, source_target_pairs={{0,8},{4,12},{8,16},{12,20},{16,24},{20,28},{24,0},{28,4},{1,9},{5... | collective-permute-start | bytes 1966088 | tf_op jit(solution)/shard_map/ppermute | solution.py:24
  71.1 50.3 %collective-permute-start.10 = (f32[1280,128]{1,0:T(8,128)}, f32[1280,128]{1,0:T(8,128)}, u32[]{:S(2)}, u32[]{:S(2)}) collective-permute-start(f32[1280,128]{1,0:T(8,128)} %constant_dynamic-update-slice_fusion.16.refs_0_), channel_id=1, source_target_pairs={{0,4},{4,8},{8,12},{12,16},{16,20},{20,24},{24,28},{28,0},{1,5},{5... | collective-permute-start | bytes 1966088 | tf_op jit(solution)/shard_map/ppermute | solution.py:24
  180.3 29.4 %collective-permute-start.25 = (f32[1280,128]{1,0:T(8,128)S(1)}, f32[1280,128]{1,0:T(8,128)S(1)}, u32[]{:S(2)}, u32[]{:S(2)}) collective-permute-start(f32[1280,128]{1,0:T(8,128)S(1)} %constant_dynamic-update-slice_fusion.23.refs_0_), channel_id=1, source_target_pairs={{0,24},{4,28},{8,0},{12,4},{16,8},{20,12},{24,16},{28,20},{1,25},{... | collective-permute-start | bytes 1966088 | tf_op jit(solution)/shard_map/ppermute | solution.py:24
  180.7 58.8 %collective-permute-start.23 = (f32[1280,128]{1,0:T(8,128)S(1)}, f32[1280,128]{1,0:T(8,128)S(1)}, u32[]{:S(2)}, u32[]{:S(2)}) collective-permute-start(f32[1280,128]{1,0:T(8,128)S(1)} %constant_dynamic-update-slice_fusion.23.refs_0_), channel_id=1, source_target_pairs={{0,16},{4,20},{8,24},{12,28},{16,0},{20,4},{24,8},{28,12},{1,17},{... | collective-permute-start | bytes 1966088 | tf_op jit(solution)/shard_map/ppermute | solution.py:24
  182.5 57.7 %collective-permute-start.22 = (f32[1280,128]{1,0:T(8,128)S(1)}, f32[1280,128]{1,0:T(8,128)S(1)}, u32[]{:S(2)}, u32[]{:S(2)}) collective-permute-start(f32[1280,128]{1,0:T(8,128)S(1)} %constant_dynamic-update-slice_fusion.23.refs_0_), channel_id=1, source_target_pairs={{0,12},{4,16},{8,20},{12,24},{16,28},{20,0},{24,4},{28,8},{1,13},{... | collective-permute-start | bytes 1966088 | tf_op jit(solution)/shard_map/ppermute | solution.py:24
  195.5 44.8 %collective-permute-start.21 = (f32[1280,128]{1,0:T(8,128)S(1)}, f32[1280,128]{1,0:T(8,128)S(1)}, u32[]{:S(2)}, u32[]{:S(2)}) collective-permute-start(f32[1280,128]{1,0:T(8,128)S(1)} %constant_dynamic-update-slice_fusion.23.refs_0_), channel_id=1, source_target_pairs={{0,8},{4,12},{8,16},{12,20},{16,24},{20,28},{24,0},{28,4},{1,9},{5... | collective-permute-start | bytes 1966088 | tf_op jit(solution)/shard_map/ppermute | solution.py:24
  209.7 30.5 %collective-permute-start.20 = (f32[1280,128]{1,0:T(8,128)S(1)}, f32[1280,128]{1,0:T(8,128)S(1)}, u32[]{:S(2)}, u32[]{:S(2)}) collective-permute-start(f32[1280,128]{1,0:T(8,128)S(1)} %constant_dynamic-update-slice_fusion.23.refs_0_), channel_id=1, source_target_pairs={{0,4},{4,8},{8,12},{12,16},{16,20},{20,24},{24,28},{28,0},{1,5},{5... | collective-permute-start | bytes 1966088 | tf_op jit(solution)/shard_map/ppermute | solution.py:24
  294.8 30.2 %collective-permute-start.35 = (f32[1280,128]{1,0:T(8,128)S(1)}, f32[1280,128]{1,0:T(8,128)S(1)}, u32[]{:S(2)}, u32[]{:S(2)}) collective-permute-start(f32[1280,128]{1,0:T(8,128)S(1)} %constant_dynamic-update-slice_fusion.30.refs_0_), channel_id=1, source_target_pairs={{0,24},{4,28},{8,0},{12,4},{16,8},{20,12},{24,16},{28,20},{1,25},{... | collective-permute-start | bytes 1966088 | tf_op jit(solution)/shard_map/ppermute | solution.py:24
  295.6 30.4 %collective-permute-start.34 = (f32[1280,128]{1,0:T(8,128)S(1)}, f32[1280,128]{1,0:T(8,128)S(1)}, u32[]{:S(2)}, u32[]{:S(2)}) collective-permute-start(f32[1280,128]{1,0:T(8,128)S(1)} %constant_dynamic-update-slice_fusion.30.refs_0_), channel_id=1, source_target_pairs={{0,20},{4,24},{8,28},{12,0},{16,4},{20,8},{24,12},{28,16},{1,21},{... | collective-permute-start | bytes 1966088 | tf_op jit(solution)/shard_map/ppermute | solution.py:24
  296.0 57.9 %collective-permute-start.33 = (f32[1280,128]{1,0:T(8,128)S(1)}, f32[1280,128]{1,0:T(8,128)S(1)}, u32[]{:S(2)}, u32[]{:S(2)}) collective-permute-start(f32[1280,128]{1,0:T(8,128)S(1)} %constant_dynamic-update-slice_fusion.30.refs_0_), channel_id=1, source_target_pairs={{0,16},{4,20},{8,24},{12,28},{16,0},{20,4},{24,8},{28,12},{1,17},{... | collective-permute-start | bytes 1966088 | tf_op jit(solution)/shard_map/ppermute | solution.py:24
  297.4 57.7 %collective-permute-start.32 = (f32[1280,128]{1,0:T(8,128)S(1)}, f32[1280,128]{1,0:T(8,128)S(1)}, u32[]{:S(2)}, u32[]{:S(2)}) collective-permute-start(f32[1280,128]{1,0:T(8,128)S(1)} %constant_dynamic-update-slice_fusion.30.refs_0_), channel_id=1, source_target_pairs={{0,12},{4,16},{8,20},{12,24},{16,28},{20,0},{24,4},{28,8},{1,13},{... | collective-permute-start | bytes 1966088 | tf_op jit(solution)/shard_map/ppermute | solution.py:24
  310.0 45.1 %collective-permute-start.31 = (f32[1280,128]{1,0:T(8,128)S(1)}, f32[1280,128]{1,0:T(8,128)S(1)}, u32[]{:S(2)}, u32[]{:S(2)}) collective-permute-start(f32[1280,128]{1,0:T(8,128)S(1)} %constant_dynamic-update-slice_fusion.30.refs_0_), channel_id=1, source_target_pairs={{0,8},{4,12},{8,16},{12,20},{16,24},{20,28},{24,0},{28,4},{1,9},{5... | collective-permute-start | bytes 1966088 | tf_op jit(solution)/shard_map/ppermute | solution.py:24
  325.0 30.1 %collective-permute-start.30 = (f32[1280,128]{1,0:T(8,128)S(1)}, f32[1280,128]{1,0:T(8,128)S(1)}, u32[]{:S(2)}, u32[]{:S(2)}) collective-permute-start(f32[1280,128]{1,0:T(8,128)S(1)} %constant_dynamic-update-slice_fusion.30.refs_0_), channel_id=1, source_target_pairs={{0,4},{4,8},{8,12},{12,16},{16,20},{20,24},{24,28},{28,0},{1,5},{5... | collective-permute-start | bytes 1966088 | tf_op jit(solution)/shard_map/ppermute | solution.py:24
  409.0 30.5 %collective-permute-start.44 = (f32[1280,128]{1,0:T(8,128)S(1)}, f32[1280,128]{1,0:T(8,128)S(1)}, u32[]{:S(2)}, u32[]{:S(2)}) collective-permute-start(f32[1280,128]{1,0:T(8,128)S(1)} %constant_dynamic-update-slice_fusion.37.refs_0_), channel_id=1, source_target_pairs={{0,20},{4,24},{8,28},{12,0},{16,4},{20,8},{24,12},{28,16},{1,21},{... | collective-permute-start | bytes 1966088 | tf_op jit(solution)/shard_map/ppermute | solution.py:24
  409.9 57.3 %collective-permute-start.43 = (f32[1280,128]{1,0:T(8,128)S(1)}, f32[1280,128]{1,0:T(8,128)S(1)}, u32[]{:S(2)}, u32[]{:S(2)}) collective-permute-start(f32[1280,128]{1,0:T(8,128)S(1)} %constant_dynamic-update-slice_fusion.37.refs_0_), channel_id=1, source_target_pairs={{0,16},{4,20},{8,24},{12,28},{16,0},{20,4},{24,8},{28,12},{1,17},{... | collective-permute-start | bytes 1966088 | tf_op jit(solution)/shard_map/ppermute | solution.py:24
  410.8 57.7 %collective-permute-start.42 = (f32[1280,128]{1,0:T(8,128)S(1)}, f32[1280,128]{1,0:T(8,128)S(1)}, u32[]{:S(2)}, u32[]{:S(2)}) collective-permute-start(f32[1280,128]{1,0:T(8,128)S(1)} %constant_dynamic-update-slice_fusion.37.refs_0_), channel_id=1, source_target_pairs={{0,12},{4,16},{8,20},{12,24},{16,28},{20,0},{24,4},{28,8},{1,13},{... | collective-permute-start | bytes 1966088 | tf_op jit(solution)/shard_map/ppermute | solution.py:24
  423.4 45.2 %collective-permute-start.41 = (f32[1280,128]{1,0:T(8,128)S(1)}, f32[1280,128]{1,0:T(8,128)S(1)}, u32[]{:S(2)}, u32[]{:S(2)}) collective-permute-start(f32[1280,128]{1,0:T(8,128)S(1)} %constant_dynamic-update-slice_fusion.37.refs_0_), channel_id=1, source_target_pairs={{0,8},{4,12},{8,16},{12,20},{16,24},{20,28},{24,0},{28,4},{1,9},{5... | collective-permute-start | bytes 1966088 | tf_op jit(solution)/shard_map/ppermute | solution.py:24
  437.4 31.1 %collective-permute-start.40 = (f32[1280,128]{1,0:T(8,128)S(1)}, f32[1280,128]{1,0:T(8,128)S(1)}, u32[]{:S(2)}, u32[]{:S(2)}) collective-permute-start(f32[1280,128]{1,0:T(8,128)S(1)} %constant_dynamic-update-slice_fusion.37.refs_0_), channel_id=1, source_target_pairs={{0,4},{4,8},{8,12},{12,16},{16,20},{20,24},{24,28},{28,0},{1,5},{5... | collective-permute-start | bytes 1966088 | tf_op jit(solution)/shard_map/ppermute | solution.py:24
  502.2 29.3 %collective-permute-start.47 = (f32[416,128]{1,0:T(8,128)S(1)}, f32[416,128]{1,0:T(8,128)S(1)}, u32[]{:S(2)}, u32[]{:S(2)}) collective-permute-start(f32[416,128]{1,0:T(8,128)S(1)} %constant_dynamic-update-slice_fusion.42), channel_id=1, source_target_pairs={{0,1},{1,2},{2,3},{3,0},{4,5},{5,6},{6,7},{7,4},{8,9},{9,10},{10,1... | collective-permute-start | bytes 638984 | tf_op jit(solution)/shard_map/ppermute | solution.py:24
  543.5 30.2 %collective-permute-start.54 = (f32[1280,128]{1,0:T(8,128)S(1)}, f32[1280,128]{1,0:T(8,128)S(1)}, u32[]{:S(2)}, u32[]{:S(2)}) collective-permute-start(f32[1280,128]{1,0:T(8,128)S(1)} %constant_dynamic-update-slice_fusion.44.refs_0_), channel_id=1, source_target_pairs={{0,20},{4,24},{8,28},{12,0},{16,4},{20,8},{24,12},{28,16},{1,21},{... | collective-permute-start | bytes 1966088 | tf_op jit(solution)/shard_map/ppermute | solution.py:24
  544.1 57.6 %collective-permute-start.53 = (f32[1280,128]{1,0:T(8,128)S(1)}, f32[1280,128]{1,0:T(8,128)S(1)}, u32[]{:S(2)}, u32[]{:S(2)}) collective-permute-start(f32[1280,128]{1,0:T(8,128)S(1)} %constant_dynamic-update-slice_fusion.44.refs_0_), channel_id=1, source_target_pairs={{0,16},{4,20},{8,24},{12,28},{16,0},{20,4},{24,8},{28,12},{1,17},{... | collective-permute-start | bytes 1966088 | tf_op jit(solution)/shard_map/ppermute | solution.py:24
  545.2 57.7 %collective-permute-start.52 = (f32[1280,128]{1,0:T(8,128)S(1)}, f32[1280,128]{1,0:T(8,128)S(1)}, u32[]{:S(2)}, u32[]{:S(2)}) collective-permute-start(f32[1280,128]{1,0:T(8,128)S(1)} %constant_dynamic-update-slice_fusion.44.refs_0_), channel_id=1, source_target_pairs={{0,12},{4,16},{8,20},{12,24},{16,28},{20,0},{24,4},{28,8},{1,13},{... | collective-permute-start | bytes 1966088 | tf_op jit(solution)/shard_map/ppermute | solution.py:24
  557.4 45.4 %collective-permute-start.51 = (f32[1280,128]{1,0:T(8,128)S(1)}, f32[1280,128]{1,0:T(8,128)S(1)}, u32[]{:S(2)}, u32[]{:S(2)}) collective-permute-start(f32[1280,128]{1,0:T(8,128)S(1)} %constant_dynamic-update-slice_fusion.44.refs_0_), channel_id=1, source_target_pairs={{0,8},{4,12},{8,16},{12,20},{16,24},{20,28},{24,0},{28,4},{1,9},{5... | collective-permute-start | bytes 1966088 | tf_op jit(solution)/shard_map/ppermute | solution.py:24
  571.5 31.4 %collective-permute-start.50 = (f32[1280,128]{1,0:T(8,128)S(1)}, f32[1280,128]{1,0:T(8,128)S(1)}, u32[]{:S(2)}, u32[]{:S(2)}) collective-permute-start(f32[1280,128]{1,0:T(8,128)S(1)} %constant_dynamic-update-slice_fusion.44.refs_0_), channel_id=1, source_target_pairs={{0,4},{4,8},{8,12},{12,16},{16,20},{20,24},{24,28},{28,0},{1,5},{5... | collective-permute-start | bytes 1966088 | tf_op jit(solution)/shard_map/ppermute | solution.py:24
  659.6 30.9 %collective-permute-start.65 = (f32[1280,128]{1,0:T(8,128)S(1)}, f32[1280,128]{1,0:T(8,128)S(1)}, u32[]{:S(2)}, u32[]{:S(2)}) collective-permute-start(f32[1280,128]{1,0:T(8,128)S(1)} %constant_dynamic-update-slice_fusion.51.refs_0_), channel_id=1, source_target_pairs={{0,24},{4,28},{8,0},{12,4},{16,8},{20,12},{24,16},{28,20},{1,25},{... | collective-permute-start | bytes 1966088 | tf_op jit(solution)/shard_map/ppermute | solution.py:24
  662.1 57.6 %collective-permute-start.63 = (f32[1280,128]{1,0:T(8,128)S(1)}, f32[1280,128]{1,0:T(8,128)S(1)}, u32[]{:S(2)}, u32[]{:S(2)}) collective-permute-start(f32[1280,128]{1,0:T(8,128)S(1)} %constant_dynamic-update-slice_fusion.51.refs_0_), channel_id=1, source_target_pairs={{0,16},{4,20},{8,24},{12,28},{16,0},{20,4},{24,8},{28,12},{1,17},{... | collective-permute-start | bytes 1966088 | tf_op jit(solution)/shard_map/ppermute | solution.py:24
  663.0 57.6 %collective-permute-start.62 = (f32[1280,128]{1,0:T(8,128)S(1)}, f32[1280,128]{1,0:T(8,128)S(1)}, u32[]{:S(2)}, u32[]{:S(2)}) collective-permute-start(f32[1280,128]{1,0:T(8,128)S(1)} %constant_dynamic-update-slice_fusion.51.refs_0_), channel_id=1, source_target_pairs={{0,12},{4,16},{8,20},{12,24},{16,28},{20,0},{24,4},{28,8},{1,13},{... | collective-permute-start | bytes 1966088 | tf_op jit(solution)/shard_map/ppermute | solution.py:24
  674.4 46.2 %collective-permute-start.61 = (f32[1280,128]{1,0:T(8,128)S(1)}, f32[1280,128]{1,0:T(8,128)S(1)}, u32[]{:S(2)}, u32[]{:S(2)}) collective-permute-start(f32[1280,128]{1,0:T(8,128)S(1)} %constant_dynamic-update-slice_fusion.51.refs_0_), channel_id=1, source_target_pairs={{0,8},{4,12},{8,16},{12,20},{16,24},{20,28},{24,0},{28,4},{1,9},{5... | collective-permute-start | bytes 1966088 | tf_op jit(solution)/shard_map/ppermute | solution.py:24
  690.5 30.1 %collective-permute-start.60 = (f32[1280,128]{1,0:T(8,128)S(1)}, f32[1280,128]{1,0:T(8,128)S(1)}, u32[]{:S(2)}, u32[]{:S(2)}) collective-permute-start(f32[1280,128]{1,0:T(8,128)S(1)} %constant_dynamic-update-slice_fusion.51.refs_0_), channel_id=1, source_target_pairs={{0,4},{4,8},{8,12},{12,16},{16,20},{20,24},{24,28},{28,0},{1,5},{5... | collective-permute-start | bytes 1966088 | tf_op jit(solution)/shard_map/ppermute | solution.py:24
  (104 other events, 2212.0 us)
